TPU v7x, 32 devices: a whole 2x2x4 slice. The times are simulated.
32 devices in a mesh: virt: 8 (over z, x), pair: 4 (over y, core).
Axes of the slice: x: 2, y: 2, z: 4, core: 2. Of those that a mesh axis runs over, the one named last changes fastest.
Arguments:
- amplitudes: bfloat16 [8, 1024, 2, 1024], P('pair'), may hold values from -6 to 6
- integrals: bfloat16 [2, 512, 8, 65536], P(None, None, None, ('virt', 'pair')), may hold values from -0.125 to 0.125
- virt_counts: int32 [8], replicated, may hold values from 32 to 64, as said below
- pair_counts: int32 [8], replicated, may hold values from 512 to 1024, as said below
- pair_list: int32 [8, 1024, 2], P('pair'), may hold values from 0 to 99
- eps_occ: float32 [100], replicated, may hold values from -2 to -0.3
- eps_virt: float32 [512], replicated, may hold values from 0.3 to 4
Outputs:
- update: bfloat16 [8, 1024, 32768], P('pair', None, 'virt')
- pair_energy: float32 [8, 1024], P('pair', 'virt')
Inputs may be any that keep to these rules, and one draw needn't show every extreme that they name: virt_counts[0] = 64; every count is at least 32. `pair_counts`: some pair symmetry has exactly 1024 pairs; every count is at least 512.
All inputs are finite; a program needn't handle non-finite values.
Results may differ from a plain program's by a relative error of at most 0.001.
Values may be sent and summed in bfloat16 or wider, within the bound.
A program may use at most 192 MiB of HBM per device.

v0:
```python
import functools

import jax
import jax.numpy as jnp
from jax import lax
from jax.experimental import pallas as pl
from jax.experimental.pallas import tpu as pltpu
from jax.sharding import PartitionSpec as P

IRREPS = 8
NV = 512
BLK = 64
CS = 16
SLABS = 2
A_SORT = 32
MESH = pl.DeviceIdType.MESH


def pick_counts(irrep_ids, table):
    onehot = irrep_ids[..., None] == jnp.arange(table.shape[0], dtype=jnp.int32)
    return jnp.sum(jnp.where(onehot, table, 0), axis=-1)


def shards(amplitudes, integrals, virt_counts, pair_counts, pair_list, eps_occ, eps_virt):
    local_irreps = amplitudes.shape[0]
    rows = amplitudes.shape[1]
    width = amplitudes.shape[3]
    n_virt = lax.axis_size("virt")
    n_pair = lax.axis_size("pair")
    a_local = NV // n_virt
    irrep_ids = lax.axis_index("pair") * local_irreps + jnp.arange(local_irreps, dtype=jnp.int32)
    slots = jnp.arange(BLK, dtype=jnp.int32)
    live_d = slots[None, :] < pick_counts(irrep_ids, virt_counts)[:, None]
    dmask = jnp.tile(live_d, (1, CS)).astype(jnp.bfloat16)
    masked = amplitudes * dmask[:, None, None, :]
    ladder = jnp.zeros((local_irreps, rows, a_local, BLK), jnp.float32)
    for s in range(SLABS):
        piece = integrals[s]
        moved = lax.all_to_all(
            lax.all_to_all(piece, "virt", split_axis=0, concat_axis=2, tiled=True),
            "pair",
            split_axis=1,
            concat_axis=2,
            tiled=True,
        )
        moved = moved.reshape(a_local, local_irreps, n_pair, n_virt, -1)
        moved = jnp.transpose(moved, (0, 1, 3, 2, 4)).reshape(a_local, local_irreps, BLK, width)
        ladder = ladder + jnp.einsum(
            "hrk,ahsk->hras", masked[:, :, s, :], moved, preferred_element_type=jnp.float32
        )
    a_global = lax.axis_index("virt") * a_local + jnp.arange(a_local, dtype=jnp.int32)
    a_irrep = a_global // BLK
    a_slot = a_global % BLK
    live_a = a_slot < pick_counts(a_irrep, virt_counts)
    eps_a = lax.dynamic_slice_in_dim(eps_virt, lax.axis_index("virt") * a_local, a_local)
    b_irrep = jnp.bitwise_xor(a_irrep[None, :], irrep_ids[:, None])
    b_onehot = (b_irrep[..., None] == jnp.arange(IRREPS, dtype=jnp.int32)).astype(jnp.float32)
    eps_table = eps_virt.reshape(IRREPS, BLK)
    eps_b = jnp.einsum("hag,gs->has", b_onehot, eps_table, precision=lax.Precision.HIGHEST)
    live_b = slots[None, None, :] < pick_counts(b_irrep, virt_counts)[..., None]
    occ_onehot = pair_list[..., None] == jnp.arange(eps_occ.shape[0], dtype=jnp.int32)
    occ_terms = jnp.sum(jnp.where(occ_onehot, eps_occ, 0.0), axis=-1)
    occ = occ_terms[:, :, 0] + occ_terms[:, :, 1]
    live_rows = (
        jnp.arange(rows, dtype=jnp.int32)[None, :] < pick_counts(irrep_ids, pair_counts)[:, None]
    )
    denom = (eps_a[None, :, None] + eps_b)[:, None, :, :] - occ[:, :, None, None]
    live = live_rows[:, :, None, None] & live_a[None, None, :, None] & live_b[:, None, :, :]
    ratio = jnp.where(live, ladder / denom, jnp.zeros_like(ladder))
    update = ratio.astype(jnp.bfloat16).reshape(local_irreps, rows, a_local * BLK)
    partial_value = jnp.sum(ratio * ladder, axis=(2, 3)) / (NV * BLK)
    energy = lax.psum_scatter(partial_value, "virt", scatter_dimension=1, tiled=True)
    return (update, energy)


def flip_bits(index, pattern, count):
    flipped = 0
    weight = 1
    while weight < count:
        bit = (index // weight) % 2
        mine = (pattern // weight) % 2
        flipped = flipped + weight * (bit + mine - 2 * bit * mine)
        weight *= 2
    return flipped


def send_order(count):
    half, quarter = count // 2, count // 4
    far = list(range(count - 1, half - 1, -1))
    near = list(range(half - 1, -1, -1))
    mixed = [d for both in zip(far[:quarter], near[:quarter]) for d in both]
    return mixed + far[quarter:] + near[quarter:]


def ladder_kernel(
    n_virt, n_pair, irreps_here, a_chunk, cuts, depth, parts_sb, energy_scale,
    eri_ref, amps_ref, dmask_ref, rows_ref, occ_ref, sort_in_ref, sort_out_ref,
    got_ref, recv_ref, energy_ref,
    x_buf, stage, y_buf, out_buf, terms, parts,
    x_sem, y_sem, own_sem, keep_sem, send_sem, recv_sem, out_sem, got_sem, term_sem, part_sem,
):
    me_v = lax.axis_index("virt")
    me_p = lax.axis_index("pair")
    slabs = eri_ref.shape[0]
    loc = eri_ref.shape[2]
    irreps = irreps_here * n_pair
    ks = amps_ref.shape[2]
    nrows = amps_ref.shape[3]
    sort_rows = sort_in_ref.shape[0]
    a_sort = sort_rows // irreps
    sb_here = n_pair * parts_sb
    chunk_rows = a_chunk * irreps
    steps = n_virt * cuts
    order = send_order(n_virt)
    e_cols = nrows // n_virt
    tile_n = 512
    tile_r = 256

    barrier = pltpu.get_barrier_semaphore()
    for d in range(1, n_pair):
        pl.semaphore_signal(barrier, inc=1, device_id=(me_v, flip_bits(me_p, d, n_pair)), device_id_type=MESH)
    for d in range(1, n_virt):
        pl.semaphore_signal(barrier, inc=1, device_id=(flip_bits(me_v, d, n_virt), me_p), device_id_type=MESH)
    pl.semaphore_wait(barrier, n_pair - 1 + n_virt - 1)

    def target(t):
        return flip_bits(me_v, order[t // cuts], n_virt)

    def pair_copy(t, d):
        peer = flip_bits(me_p, d, n_pair)
        return pltpu.make_async_remote_copy(
            src_ref=stage.at[t % depth, peer],
            dst_ref=recv_ref.at[t, me_p],
            send_sem=send_sem.at[t % depth, d - 1],
            recv_sem=recv_sem.at[t, d - 1],
            device_id=(me_v, peer),
            device_id_type=MESH,
        )

    def own_copy(t):
        return pltpu.make_async_copy(stage.at[t % depth, me_p], recv_ref.at[t, me_p], own_sem.at[t % depth])

    def out_copy(t):
        dest = target(t)
        cut = t % cuts
        there = got_ref.at[:, cut * a_chunk : (cut + 1) * a_chunk, me_v]
        if order[t // cuts] == 0:
            return pltpu.make_async_copy(out_buf.at[t], there, keep_sem.at[cut])
        return pltpu.make_async_remote_copy(
            src_ref=out_buf.at[t],
            dst_ref=there,
            send_sem=out_sem.at[t],
            recv_sem=got_sem.at[t],
            device_id=(dest, me_p),
            device_id_type=MESH,
        )

    def part_copy(d):
        dest = flip_bits(me_v, d, n_virt)
        cols = pl.ds(pl.multiple_of(dest * e_cols, e_cols), e_cols)
        return pltpu.make_async_remote_copy(
            src_ref=terms.at[:, cols],
            dst_ref=parts.at[d - 1],
            send_sem=term_sem.at[d - 1],
            recv_sem=part_sem.at[d - 1],
            device_id=(dest, me_p),
            device_id_type=MESH,
        )

    def prepare(t):
        dest = target(t)
        load = pltpu.make_async_copy(
            eri_ref.at[:, pl.ds(pl.multiple_of((dest * cuts + t % cuts) * chunk_rows, chunk_rows), chunk_rows), :], x_buf, x_sem
        )
        load.start()
        load.wait()

        def sort_tile(n, carry):
            cols = pl.ds(pl.multiple_of(n * tile_n, tile_n), tile_n)
            for s in range(slabs):
                for q in range(a_chunk // a_sort):
                    block = x_buf[s, q * sort_rows : (q + 1) * sort_rows, cols]
                    sorted_rows = jnp.dot(
                        sort_in_ref[...], block, preferred_element_type=jnp.float32
                    ).astype(jnp.bfloat16)
                    for h in range(irreps):
                        stage[
                            t % depth, h // irreps_here, h % irreps_here, s, q * a_sort : (q + 1) * a_sort, cols
                        ] = sorted_rows[h * a_sort : (h + 1) * a_sort]
            return carry

        lax.fori_loop(0, loc // tile_n, sort_tile, 0)
        for d in range(1, n_pair):
            pair_copy(t, d).start()
        own_copy(t).start()

    def compute(t):
        dest = target(t)
        load = pltpu.make_async_copy(recv_ref.at[t], y_buf, y_sem)
        load.start()
        load.wait()
        for hh in range(irreps_here):

            def tile(n, carry):
                cols = pl.ds(pl.multiple_of(n * tile_r, tile_r), tile_r)
                ladder = None
                for s in range(slabs):
                    left = jnp.concatenate(
                        [
                            y_buf[p, hh, s, :, j * ks : (j + 1) * ks]
                            for p in range(n_pair)
                            for j in range(parts_sb)
                        ],
                        axis=0,
                    )
                    left = left * dmask_ref[hh : hh + 1, :]
                    term = jnp.dot(left, amps_ref[hh, s, :, cols], preferred_element_type=jnp.float32)
                    ladder = term if ladder is None else ladder + term
                base = rows_ref[dest * cuts + t % cuts, :, hh : hh + 1]
                live = rows_ref[dest * cuts + t % cuts, :, irreps_here + hh : irreps_here + hh + 1]
                occ = occ_ref[hh : hh + 1, cols]
                live_r = occ_ref[irreps_here + hh : irreps_here + hh + 1, cols]
                denom = base - occ
                ratio = jnp.where(live * live_r > 0.5, ladder / denom, 0.0)
                terms[hh : hh + 1, cols] += jnp.sum(ratio * ladder, axis=0, keepdims=True)
                update = jnp.dot(
                    sort_out_ref[...], ratio.astype(jnp.bfloat16), preferred_element_type=jnp.float32
                ).astype(jnp.bfloat16)
                out_buf[t, hh, :, :, cols] = update.reshape(a_chunk, sb_here, tile_r)
                return carry

            lax.fori_loop(0, nrows // tile_r, tile, 0)
        out_copy(t).start()

    terms[...] = jnp.zeros_like(terms)
    for t in range(depth):
        prepare(t)
    for t in range(steps):
        for d in range(1, n_pair):
            pair_copy(t, d).wait_recv()
        own_copy(t).wait()
        compute(t)
        for d in range(1, n_pair):
            pair_copy(t, d).wait_send()
        if t + depth < steps:
            prepare(t + depth)
    for d in range(1, n_virt):
        part_copy(d).start()
    for d in range(1, n_virt):
        part_copy(d).wait()
    mine = terms[:, pl.ds(pl.multiple_of(me_v * e_cols, e_cols), e_cols)]
    for d in range(1, n_virt):
        mine = mine + parts[d - 1]
    energy_ref[...] = mine / energy_scale
    for t in range(steps):
        out_copy(t).wait()


def fused_shards(amplitudes, integrals, virt_counts, pair_counts, pair_list, eps_occ, eps_virt):
    irreps_here, rows, slabs, ks = amplitudes.shape
    n_virt = lax.axis_size("virt")
    n_pair = lax.axis_size("pair")
    nv = integrals.shape[1]
    irreps = integrals.shape[2]
    loc = integrals.shape[3]
    cuts = nv // n_virt // A_SORT
    depth = 4
    a_chunk = A_SORT
    steps = n_virt * cuts
    parts_sb = loc // ks
    sb_here = n_pair * parts_sb
    me_v = lax.axis_index("virt")
    irrep_ids = lax.axis_index("pair") * irreps_here + jnp.arange(irreps_here, dtype=jnp.int32)
    slots = jnp.arange(BLK, dtype=jnp.int32)
    live_d = slots[None, :] < pick_counts(irrep_ids, virt_counts)[:, None]
    dmask = jnp.tile(live_d, (1, ks // BLK)).astype(jnp.bfloat16)
    amps = jnp.transpose(amplitudes, (0, 2, 3, 1))

    a_index = jnp.arange(nv, dtype=jnp.int32)
    a_irrep = a_index // BLK
    live_virt = (slots[None, :] < virt_counts[:, None]).astype(jnp.float32)
    b_irrep = jnp.bitwise_xor(a_irrep[None, :], irrep_ids[:, None])
    b_onehot = (b_irrep[..., None] == jnp.arange(irreps, dtype=jnp.int32)).astype(jnp.float32)
    eps_here = lax.dynamic_slice_in_dim(eps_virt.reshape(irreps, BLK), me_v * sb_here, sb_here, axis=1)
    live_here = lax.dynamic_slice_in_dim(live_virt, me_v * sb_here, sb_here, axis=1)
    eps_b = jnp.einsum("hag,gs->hsa", b_onehot, eps_here, precision=lax.Precision.HIGHEST)
    live_b = jnp.einsum("hag,gs->hsa", b_onehot, live_here, precision=lax.Precision.HIGHEST)
    base = eps_virt[None, None, :] + eps_b
    live = live_virt.reshape(-1)[None, None, :] * live_b
    cols = jnp.concatenate([base, live], axis=0)
    cols = cols.reshape(2 * irreps_here, sb_here, steps, a_chunk)
    cols = jnp.transpose(cols, (2, 1, 3, 0)).reshape(steps, sb_here * a_chunk, 2 * irreps_here)

    occ_onehot = pair_list[..., None] == jnp.arange(eps_occ.shape[0], dtype=jnp.int32)
    occ_terms = jnp.sum(jnp.where(occ_onehot, eps_occ, 0.0), axis=-1)
    occ = occ_terms[:, :, 0] + occ_terms[:, :, 1]
    live_rows = jnp.arange(rows, dtype=jnp.int32)[None, :] < pick_counts(irrep_ids, pair_counts)[:, None]
    occ_live = jnp.concatenate([occ, live_rows.astype(jnp.float32)], axis=0)

    a_sort = A_SORT
    n_in = a_sort * irreps
    i_in = jnp.arange(n_in, dtype=jnp.int32)
    from_in = (i_in % a_sort) * irreps + i_in // a_sort
    sort_in = (from_in[:, None] == i_in[None, :]).astype(jnp.bfloat16)
    i_out = jnp.arange(a_chunk * sb_here, dtype=jnp.int32)
    from_out = (i_out % sb_here) * a_chunk + i_out // sb_here
    sort_out = (from_out[:, None] == i_out[None, :]).astype(jnp.bfloat16)

    eri = integrals.reshape(slabs, nv * irreps, loc)
    vmem = pl.BlockSpec(memory_space=pltpu.VMEM)
    hbm = pl.BlockSpec(memory_space=pl.ANY)
    got, _, energy = pl.pallas_call(
        functools.partial(ladder_kernel, n_virt, n_pair, irreps_here, a_chunk, cuts, depth, parts_sb, nv * BLK),
        out_shape=(
            jax.ShapeDtypeStruct((irreps_here, a_chunk * cuts, n_virt, sb_here, rows), jnp.bfloat16),
            jax.ShapeDtypeStruct((steps, n_pair, irreps_here, slabs, a_chunk, loc), jnp.bfloat16),
            jax.ShapeDtypeStruct((irreps_here, rows // n_virt), jnp.float32),
        ),
        in_specs=[hbm, vmem, vmem, vmem, vmem, vmem, vmem],
        out_specs=(hbm, hbm, vmem),
        scratch_shapes=[
            pltpu.VMEM((slabs, a_chunk * irreps, loc), jnp.bfloat16),
            pltpu.VMEM((depth, n_pair, irreps_here, slabs, a_chunk, loc), jnp.bfloat16),
            pltpu.VMEM((n_pair, irreps_here, slabs, a_chunk, loc), jnp.bfloat16),
            pltpu.VMEM((steps, irreps_here, a_chunk, sb_here, rows), jnp.bfloat16),
            pltpu.VMEM((irreps_here, rows), jnp.float32),
            pltpu.VMEM((n_virt - 1, irreps_here, rows // n_virt), jnp.float32),
            pltpu.SemaphoreType.DMA,
            pltpu.SemaphoreType.DMA,
            pltpu.SemaphoreType.DMA((depth,)),
            pltpu.SemaphoreType.DMA((cuts,)),
            pltpu.SemaphoreType.DMA((depth, n_pair - 1)),
            pltpu.SemaphoreType.DMA((steps, n_pair - 1)),
            pltpu.SemaphoreType.DMA((steps,)),
            pltpu.SemaphoreType.DMA((steps,)),
            pltpu.SemaphoreType.DMA((n_virt - 1,)),
            pltpu.SemaphoreType.DMA((n_virt - 1,)),
        ],
        compiler_params=pltpu.CompilerParams(
            collective_id=0, has_side_effects=True, vmem_limit_bytes=60 * 1024 * 1024
        ),
    )(eri, amps, dmask, cols, occ_live, sort_in, sort_out)
    flat = got.reshape(irreps_here, a_chunk * cuts * BLK, rows)
    update = jnp.transpose(flat, (0, 2, 1))
    return (update, energy)


def solution(mesh):
    placed = (
        P("pair", None, None, None),
        P(None, None, None, ("virt", "pair")),
        P(),
        P(),
        P("pair", None, None),
        P(),
        P(),
    )

    def run(*arrays):
        amplitudes, integrals = arrays[:2]
        loc = integrals.shape[3] // (mesh.shape["virt"] * mesh.shape["pair"])
        whole_slots = loc % amplitudes.shape[3] == 0
        whole_chunks = (integrals.shape[1] // mesh.shape["virt"]) % A_SORT == 0
        body = fused_shards if whole_slots and whole_chunks else shards
        return jax.shard_map(
            body,
            mesh=mesh,
            in_specs=placed,
            out_specs=(P("pair", None, "virt"), P("pair", "virt")),
            check_vma=False,
        )(*arrays)

    return run
```

profile of v0, /device:TPU:0, one launch (start us, length us, event | category | flops | bytes accessed | tf_op | source)
XLA Modules:
  0.0 501.1 jit_solution(16734575661655518635)
XLA Ops:
  0.7 0.9 select_reduce_fusion
  1.6 0.1 compare_convert_fusion.1
  1.6 0.1 broadcast_xor_fusion
  1.7 0.8 reshape.151
  2.5 0.7 iota_compare_fusion.5
  3.2 0.1 reshape.155
  3.3 0.7 convert_element_type.26.dmask_ref
  4.0 0.1 compare_convert_fusion
  4.0 1.7 fusion
  5.7 0.6 pad_maximum_fusion.1.occ_ref
  6.3 0.9 fusion.2
  7.3 0.3 fusion.1
  7.6 0.1 reshape.152
  7.7 0.8 fusion.3
  8.5 2.1 copy.29
  10.7 21.0 %copy.26 = bf16[2,1024,2,1024]{1,3,2,0:T(8,128)(2,1)} copy(bf16[2,1024,2,1024]{3,2,1,0:T(2,128)(2,1)} %param.7) | data formatting | bytes 16777216 | tf_op args[0]
  31.7 447.6 %shard_map.86 = (bf16[2,64,8,8,1024]{4,3,2,1,0:T(8,128)(2,1)}, bf16[16,4,2,2,32,2048]{5,4,3,2,1,0:T(8,128)(2,1)}, f32[2,128]{1,0:T(2,128)}) custom-call(bf16[2,4096,2048]{2,1,0:T(8,128)(2,1)} %bitcast.20, bf16[2,2,1024,1024]{3,2,1,0:T(8,128)(2,1)} %bitcast.21, bf16[2,1024]{1,0:T(2,128)(2,1)} %convert_element_type.26.dmask_ref, f32[16,256,4]{2,1,0:T(8,128)} %bitcast.24, ...), custom_call_target="tpu_custom_call" | custom-call | tf_op jit(solution)/shard_map/pallas_call | solution.py:312
  479.3 0.0 copy-start
  479.3 21.2 %copy.32 = bf16[2,4096,1024]{1,2,0:T(8,128)(2,1)} copy(bf16[2,4096,1024]{2,1,0:T(8,128)(2,1)} %bitcast.23) | data formatting | bytes 33554432 | tf_op jit(solution)/shard_map/reshape | solution.py:343
  500.5 0.0 copy-done
  500.5 0.6 copy.43
  (8 shorter events, 0.1 us)
Async XLA Ops:
  479.3 21.2 %copy-start = (f32[2,128]{1,0:T(2,128)S(1)}, f32[2,128]{1,0:T(2,128)}, u32[]{:S(2)}) copy-start(f32[2,128]{1,0:T(2,128)} %get-tuple-element.17) | copy-start | bytes 3076
where the time goes:
time: 504 us; the launch traced here: 501 us
  Pallas kernels  448 us (89%)
  local copies, waits for them, and re-layouts  46.6 us (9%)
    pallas_call x1, Pallas kernels, fused_shards(): pl.pallas_call(functools.partial(ladder_kernel, n_virt, n_pair, irreps_he...  448 us
    unnamed x4, local copies, waits for them, and re-layouts  21.6 us
    reshape x1, local copies, waits for them, and re-layouts, fused_shards(): flat = got.reshape(irreps_here, a_chunk * cuts * BLK, rows)  21.2 us

commit v1 on v0

v1 whole, which is shorter than its diff:
```python
import functools

import jax
import jax.numpy as jnp
from jax import lax
from jax.experimental import pallas as pl
from jax.experimental.pallas import tpu as pltpu
from jax.sharding import PartitionSpec as P

IRREPS = 8
NV = 512
BLK = 64
CS = 16
SLABS = 2
A_UNIT = 16
MESH = pl.DeviceIdType.MESH


def pick_counts(irrep_ids, table):
    onehot = irrep_ids[..., None] == jnp.arange(table.shape[0], dtype=jnp.int32)
    return jnp.sum(jnp.where(onehot, table, 0), axis=-1)


def shards(amplitudes, integrals, virt_counts, pair_counts, pair_list, eps_occ, eps_virt):
    local_irreps = amplitudes.shape[0]
    rows = amplitudes.shape[1]
    width = amplitudes.shape[3]
    n_virt = lax.axis_size("virt")
    n_pair = lax.axis_size("pair")
    a_local = NV // n_virt
    irrep_ids = lax.axis_index("pair") * local_irreps + jnp.arange(local_irreps, dtype=jnp.int32)
    slots = jnp.arange(BLK, dtype=jnp.int32)
    live_d = slots[None, :] < pick_counts(irrep_ids, virt_counts)[:, None]
    dmask = jnp.tile(live_d, (1, CS)).astype(jnp.bfloat16)
    masked = amplitudes * dmask[:, None, None, :]
    ladder = jnp.zeros((local_irreps, rows, a_local, BLK), jnp.float32)
    for s in range(SLABS):
        piece = integrals[s]
        moved = lax.all_to_all(
            lax.all_to_all(piece, "virt", split_axis=0, concat_axis=2, tiled=True),
            "pair",
            split_axis=1,
            concat_axis=2,
            tiled=True,
        )
        moved = moved.reshape(a_local, local_irreps, n_pair, n_virt, -1)
        moved = jnp.transpose(moved, (0, 1, 3, 2, 4)).reshape(a_local, local_irreps, BLK, width)
        ladder = ladder + jnp.einsum(
            "hrk,ahsk->hras", masked[:, :, s, :], moved, preferred_element_type=jnp.float32
        )
    a_global = lax.axis_index("virt") * a_local + jnp.arange(a_local, dtype=jnp.int32)
    a_irrep = a_global // BLK
    a_slot = a_global % BLK
    live_a = a_slot < pick_counts(a_irrep, virt_counts)
    eps_a = lax.dynamic_slice_in_dim(eps_virt, lax.axis_index("virt") * a_local, a_local)
    b_irrep = jnp.bitwise_xor(a_irrep[None, :], irrep_ids[:, None])
    b_onehot = (b_irrep[..., None] == jnp.arange(IRREPS, dtype=jnp.int32)).astype(jnp.float32)
    eps_table = eps_virt.reshape(IRREPS, BLK)
    eps_b = jnp.einsum("hag,gs->has", b_onehot, eps_table, precision=lax.Precision.HIGHEST)
    live_b = slots[None, None, :] < pick_counts(b_irrep, virt_counts)[..., None]
    occ_onehot = pair_list[..., None] == jnp.arange(eps_occ.shape[0], dtype=jnp.int32)
    occ_terms = jnp.sum(jnp.where(occ_onehot, eps_occ, 0.0), axis=-1)
    occ = occ_terms[:, :, 0] + occ_terms[:, :, 1]
    live_rows = (
        jnp.arange(rows, dtype=jnp.int32)[None, :] < pick_counts(irrep_ids, pair_counts)[:, None]
    )
    denom = (eps_a[None, :, None] + eps_b)[:, None, :, :] - occ[:, :, None, None]
    live = live_rows[:, :, None, None] & live_a[None, None, :, None] & live_b[:, None, :, :]
    ratio = jnp.where(live, ladder / denom, jnp.zeros_like(ladder))
    update = ratio.astype(jnp.bfloat16).reshape(local_irreps, rows, a_local * BLK)
    partial_value = jnp.sum(ratio * ladder, axis=(2, 3)) / (NV * BLK)
    energy = lax.psum_scatter(partial_value, "virt", scatter_dimension=1, tiled=True)
    return (update, energy)


def flip_bits(index, pattern, count):
    flipped = 0
    weight = 1
    while weight < count:
        bit = (index // weight) % 2
        mine = (pattern // weight) % 2
        flipped = flipped + weight * (bit + mine - 2 * bit * mine)
        weight *= 2
    return flipped


def step_plan(count, units):
    plan = []
    for i in range(count):
        sizes = [2] * (units // 2) + [1] * (units % 2)
        if i == 0:
            sizes = [1, 1] + sizes[1:]
        if i == count - 1 and sizes[-1] == 2:
            sizes = sizes[:-1] + [1, 1]
        start = 0
        for size in sizes:
            plan.append((count - 1 - i, start, size))
            start += size
    return plan


def unit_matrix(count, outer, inner):
    rows = lax.broadcasted_iota(jnp.int32, (count * outer * inner, count * outer * inner), 0)
    cols = lax.broadcasted_iota(jnp.int32, (count * outer * inner, count * outer * inner), 1)
    unit = rows // (outer * inner)
    within = rows % (outer * inner)
    source = unit * (outer * inner) + (within % inner) * outer + within // inner
    return (source == cols).astype(jnp.float32).astype(jnp.bfloat16)


def ladder_kernel(
    n_virt, n_pair, irreps_here, depth, parts_sb, energy_scale,
    eri_ref, amps_ref, pair_ref, row_ref, vcount_ref, pcount_ref, eocc_ref, evirt_ref,
    got_ref, recv_ref, energy_ref,
    x_buf, stage, y_buf, out_buf, a_buf, amps, sort_in, sort_out, pick, levels, occ, cols_buf, terms, parts,
    x_sem, y_sem, own_sem, keep_sem, send_sem, recv_sem, out_sem, got_sem, term_sem, part_sem, a_sem,
):
    me_v = lax.axis_index("virt")
    me_p = lax.axis_index("pair")
    slabs = eri_ref.shape[0]
    loc = eri_ref.shape[2]
    irreps = irreps_here * n_pair
    ks = amps.shape[2]
    nrows = amps.shape[3]
    nv = row_ref.shape[1]
    nocc = eocc_ref.shape[0]
    a_local = nv // n_virt
    unit_rows = A_UNIT * irreps
    sb_here = n_pair * parts_sb
    out_rows = A_UNIT * sb_here
    plan = step_plan(n_virt, a_local // A_UNIT)
    steps = len(plan)
    e_cols = nrows // n_virt
    tile_n = 512
    tile_r = 256
    a_rows = a_buf.shape[1]
    peers = [d for d in range(2, n_pair)] + [1]
    first_unit = []
    total = 0
    for _, _, size in plan:
        first_unit.append(total)
        total += size

    def target(t):
        return flip_bits(me_v, plan[t][0], n_virt)

    def x_copy(t):
        _, start, size = plan[t]
        at = pl.multiple_of((target(t) * (a_local // A_UNIT) + start) * unit_rows, unit_rows)
        return pltpu.make_async_copy(
            eri_ref.at[:, pl.ds(at, size * unit_rows), :], x_buf.at[:, 0 : size * unit_rows, :], x_sem
        )

    def a_copy(block):
        per = nrows // a_rows
        at = pl.multiple_of((block % per) * a_rows, a_rows)
        return pltpu.make_async_copy(
            amps_ref.at[block // per, pl.ds(at, a_rows)], a_buf.at[block % 2], a_sem.at[block % 2]
        )

    def pair_copy(t, d):
        peer = flip_bits(me_p, d, n_pair)
        size = plan[t][2]
        return pltpu.make_async_remote_copy(
            src_ref=stage.at[t % depth, 0:size, peer],
            dst_ref=recv_ref.at[first_unit[t] : first_unit[t] + size, me_p],
            send_sem=send_sem.at[t % depth, d - 1],
            recv_sem=recv_sem.at[t, d - 1],
            device_id=(me_v, peer),
            device_id_type=MESH,
        )

    def own_copy(t):
        size = plan[t][2]
        return pltpu.make_async_copy(
            stage.at[t % depth, 0:size, me_p],
            recv_ref.at[first_unit[t] : first_unit[t] + size, me_p],
            own_sem.at[t % depth],
        )

    def out_copy(t, hh):
        d, start, size = plan[t]
        here = out_buf.at[first_unit[t] : first_unit[t] + size, hh]
        there = got_ref.at[hh, start : start + size, :, me_v]
        if d == 0:
            return pltpu.make_async_copy(here, there, keep_sem.at[t - (steps - keep_sem.shape[0]), hh])
        return pltpu.make_async_remote_copy(
            src_ref=here,
            dst_ref=there,
            send_sem=out_sem.at[t, hh],
            recv_sem=got_sem.at[t, hh],
            device_id=(target(t), me_p),
            device_id_type=MESH,
        )

    def part_copy(d):
        dest = flip_bits(me_v, d, n_virt)
        cols = pl.ds(pl.multiple_of(dest * e_cols, e_cols), e_cols)
        return pltpu.make_async_remote_copy(
            src_ref=terms.at[:, cols],
            dst_ref=parts.at[d - 1],
            send_sem=term_sem.at[d - 1],
            recv_sem=part_sem.at[d - 1],
            device_id=(dest, me_p),
            device_id_type=MESH,
        )

    def prepare(t):
        size = plan[t][2]
        n = size * unit_rows
        x_copy(t).wait()

        def sort_tile(i, carry):
            cols = pl.ds(pl.multiple_of(i * tile_n, tile_n), tile_n)
            for s in range(slabs):
                sorted_rows = jnp.dot(
                    sort_in[0:n, 0:n], x_buf[s, 0:n, cols], preferred_element_type=jnp.float32
                ).astype(jnp.bfloat16)
                for u in range(size):
                    for h in range(irreps):
                        at = u * unit_rows + h * A_UNIT
                        stage[
                            t % depth, u, h // irreps_here, h % irreps_here, s, :, cols
                        ] = sorted_rows[at : at + A_UNIT]
            return carry

        lax.fori_loop(0, loc // tile_n, sort_tile, 0)
        if t + 1 < steps:
            x_copy(t + 1).start()
        for d in peers:
            pair_copy(t, d).start()
        own_copy(t).start()

    def load_amps(hh):
        per = nrows // a_rows
        h = me_p * irreps_here + hh
        slot = lax.broadcasted_iota(jnp.int32, (1, tile_r), 1) % BLK
        dmask = jnp.where(slot < vcount_ref[h], 1.0, 0.0).astype(jnp.bfloat16)

        def block(i, carry):
            now = hh * per + i
            a_copy(now).wait()

            @pl.when(now + 1 < irreps_here * per)
            def _():
                a_copy(now + 1).start()

            rows = pl.ds(pl.multiple_of(i * a_rows, a_rows), a_rows)
            for c in range(ks // tile_r):
                lanes = slice(c * tile_r, (c + 1) * tile_r)
                mixed = a_buf[now % 2, :, :, lanes].reshape(a_rows * slabs, tile_r)
                split = jnp.dot(pick[0], mixed, preferred_element_type=jnp.float32).astype(jnp.bfloat16) * dmask
                turned = lax.dot_general(
                    pick[1], split, (((1,), (1,)), ((), ())), preferred_element_type=jnp.float32
                ).astype(jnp.bfloat16)
                for s in range(slabs):
                    amps[hh, s, lanes, rows] = turned[:, s * a_rows : (s + 1) * a_rows]
            return carry

        lax.fori_loop(0, per, block, 0)

    def fetch(t):
        size = plan[t][2]
        for d in range(1, n_pair):
            pair_copy(t, d).wait_recv()
        own_copy(t).wait()
        load = pltpu.make_async_copy(
            recv_ref.at[first_unit[t] : first_unit[t] + size], y_buf.at[0:size], y_sem
        )
        load.start()
        load.wait()

    def compute(t, hh):
        _, start, size = plan[t]
        n = size * out_rows
        h = me_p * irreps_here + hh
        bases = []
        lives = []
        for u in range(size):
            a_first = target(t) * a_local + (start + u) * A_UNIT
            a_irrep = a_first // BLK
            b_irrep = flip_bits(a_irrep, h, irreps)
            eps_a = levels[pl.ds(pl.multiple_of(a_first, A_UNIT), A_UNIT), 0:1]
            a_slot = a_first % BLK + lax.broadcasted_iota(jnp.int32, (A_UNIT, 1), 0)
            live_a = jnp.where(a_slot < vcount_ref[a_irrep], 1.0, 0.0)
            for b in range(sb_here):
                b_slot = me_v * sb_here + b
                bases.append(eps_a + evirt_ref[b_irrep * BLK + b_slot])
                lives.append(live_a * jnp.where(b_slot < vcount_ref[b_irrep], 1.0, 0.0))
        cols_buf[0, 0:n, :] = jnp.concatenate(bases, axis=0)
        cols_buf[1, 0:n, :] = jnp.concatenate(lives, axis=0)

        def tile(i, carry):
            cols = pl.ds(pl.multiple_of(i * tile_r, tile_r), tile_r)
            ladder = None
            for s in range(slabs):
                left = jnp.concatenate(
                    [
                        y_buf[u, p, hh, s, :, j * ks : (j + 1) * ks]
                        for u in range(size)
                        for p in range(n_pair)
                        for j in range(parts_sb)
                    ],
                    axis=0,
                )
                term = jnp.dot(left, amps[hh, s, :, cols], preferred_element_type=jnp.float32)
                ladder = term if ladder is None else ladder + term
            denom = cols_buf[0, 0:n, :] - occ[hh : hh + 1, cols]
            live = cols_buf[1, 0:n, :] * occ[irreps_here + hh : irreps_here + hh + 1, cols]
            ratio = jnp.where(live > 0.5, ladder / denom, 0.0)
            terms[hh : hh + 1, cols] += jnp.sum(ratio * ladder, axis=0, keepdims=True)
            update = jnp.dot(
                sort_out[0:n, 0:n], ratio.astype(jnp.bfloat16), preferred_element_type=jnp.float32
            ).astype(jnp.bfloat16)
            out_buf[first_unit[t] : first_unit[t] + size, hh, :, :, cols] = update.reshape(
                size, A_UNIT, sb_here, tile_r
            )
            return carry

        lax.fori_loop(0, nrows // tile_r, tile, 0)
        out_copy(t, hh).start()

    def tables():
        sort_out[...] = unit_matrix(2, A_UNIT, sb_here)
        for i in range(nv // 128):
            piece = jnp.broadcast_to(row_ref[0:1, i * 128 : (i + 1) * 128], (128, 128))
            levels[i * 128 : (i + 1) * 128, :] = piece.T
        index = pair_ref[...]

        def add_level(o, acc):
            return acc + jnp.where(index == o, eocc_ref[o], 0.0)

        picked = lax.fori_loop(0, nocc, add_level, jnp.zeros(index.shape, jnp.float32))
        slot = lax.broadcasted_iota(jnp.int32, (1, nrows), 1)
        for hh in range(irreps_here):
            occ[hh : hh + 1, :] = picked[hh, 0:1, :] + picked[hh, 1:2, :]
            live = slot < pcount_ref[me_p * irreps_here + hh]
            occ[irreps_here + hh : irreps_here + hh + 1, :] = jnp.where(live, 1.0, 0.0)
        pick[0] = unit_matrix(1, slabs, a_rows)
        pick[1] = unit_matrix(1, 1, tile_r)
        terms[...] = jnp.zeros_like(terms)

    x_copy(0).start()
    a_copy(0).start()
    barrier = pltpu.get_barrier_semaphore()
    for d in range(1, n_pair):
        pl.semaphore_signal(barrier, inc=1, device_id=(me_v, flip_bits(me_p, d, n_pair)), device_id_type=MESH)
    for d in range(1, n_virt):
        pl.semaphore_signal(barrier, inc=1, device_id=(flip_bits(me_v, d, n_virt), me_p), device_id_type=MESH)
    sort_in[...] = unit_matrix(2, irreps, A_UNIT)
    pl.semaphore_wait(barrier, n_pair - 1 + n_virt - 1)

    ahead = 0
    while ahead < 2:
        prepare(ahead)
        ahead += 1
    tables()
    for hh in range(irreps_here):
        load_amps(hh)
        if hh == 0:
            fetch(0)
        compute(0, hh)
        if ahead < depth:
            prepare(ahead)
            ahead += 1
    while ahead < depth:
        prepare(ahead)
        ahead += 1
    for t in range(steps):
        if t > 0:
            fetch(t)
            for hh in range(irreps_here):
                compute(t, hh)
        for d in range(1, n_pair):
            pair_copy(t, d).wait_send()
        if t + depth < steps:
            prepare(t + depth)
    for d in range(1, n_virt):
        part_copy(d).start()
    for d in range(1, n_virt):
        part_copy(d).wait()
    mine = terms[:, pl.ds(pl.multiple_of(me_v * e_cols, e_cols), e_cols)]
    for d in range(1, n_virt):
        mine = mine + parts[d - 1]
    energy_ref[...] = mine / energy_scale
    for t in range(steps):
        for hh in range(irreps_here):
            out_copy(t, hh).wait()


def turn_kernel(in_ref, out_ref):
    size = 256
    eye = unit_matrix(1, 1, size)
    for i in range(in_ref.shape[1] // size):
        for j in range(in_ref.shape[2] // size):
            block = in_ref[0, i * size : (i + 1) * size, j * size : (j + 1) * size]
            out_ref[0, j * size : (j + 1) * size, i * size : (i + 1) * size] = lax.dot_general(
                eye, block, (((1,), (1,)), ((), ())), preferred_element_type=jnp.float32
            ).astype(jnp.bfloat16)


def fused_shards(amplitudes, integrals, virt_counts, pair_counts, pair_list, eps_occ, eps_virt):
    irreps_here, rows, slabs, ks = amplitudes.shape
    n_virt = lax.axis_size("virt")
    n_pair = lax.axis_size("pair")
    nv = integrals.shape[1]
    irreps = integrals.shape[2]
    loc = integrals.shape[3]
    depth = 4
    a_local = nv // n_virt
    units = a_local // A_UNIT
    plan = step_plan(n_virt, units)
    steps = len(plan)
    kept = sum(1 for d, _, _ in plan if d == 0)
    parts_sb = loc // ks
    sb_here = n_pair * parts_sb
    a_rows = 256 // slabs

    eri = integrals.reshape(slabs, nv * irreps, loc)
    pairs = jnp.transpose(pair_list, (0, 2, 1))
    vmem = pl.BlockSpec(memory_space=pltpu.VMEM)
    smem = pl.BlockSpec(memory_space=pltpu.SMEM)
    hbm = pl.BlockSpec(memory_space=pl.ANY)
    got, _, energy = pl.pallas_call(
        functools.partial(ladder_kernel, n_virt, n_pair, irreps_here, depth, parts_sb, nv * BLK),
        out_shape=(
            jax.ShapeDtypeStruct((irreps_here, units, A_UNIT, n_virt, sb_here, rows), jnp.bfloat16),
            jax.ShapeDtypeStruct((units * n_virt, n_pair, irreps_here, slabs, A_UNIT, loc), jnp.bfloat16),
            jax.ShapeDtypeStruct((irreps_here, rows // n_virt), jnp.float32),
        ),
        in_specs=[hbm, hbm, vmem, vmem, smem, smem, smem, smem],
        out_specs=(hbm, hbm, vmem),
        scratch_shapes=[
            pltpu.VMEM((slabs, 2 * A_UNIT * irreps, loc), jnp.bfloat16),
            pltpu.VMEM((depth, 2, n_pair, irreps_here, slabs, A_UNIT, loc), jnp.bfloat16),
            pltpu.VMEM((2, n_pair, irreps_here, slabs, A_UNIT, loc), jnp.bfloat16),
            pltpu.VMEM((units * n_virt, irreps_here, A_UNIT, sb_here, rows), jnp.bfloat16),
            pltpu.VMEM((2, a_rows, slabs, ks), jnp.bfloat16),
            pltpu.VMEM((irreps_here, slabs, ks, rows), jnp.bfloat16),
            pltpu.VMEM((2 * A_UNIT * irreps, 2 * A_UNIT * irreps), jnp.bfloat16),
            pltpu.VMEM((2 * A_UNIT * sb_here, 2 * A_UNIT * sb_here), jnp.bfloat16),
            pltpu.VMEM((2, 256, 256), jnp.bfloat16),
            pltpu.VMEM((nv, 128), jnp.float32),
            pltpu.VMEM((2 * irreps_here, rows), jnp.float32),
            pltpu.VMEM((2, 2 * A_UNIT * sb_here, 1), jnp.float32),
            pltpu.VMEM((irreps_here, rows), jnp.float32),
            pltpu.VMEM((n_virt - 1, irreps_here, rows // n_virt), jnp.float32),
            pltpu.SemaphoreType.DMA,
            pltpu.SemaphoreType.DMA,
            pltpu.SemaphoreType.DMA((depth,)),
            pltpu.SemaphoreType.DMA((kept, irreps_here)),
            pltpu.SemaphoreType.DMA((depth, n_pair - 1)),
            pltpu.SemaphoreType.DMA((steps, n_pair - 1)),
            pltpu.SemaphoreType.DMA((steps, irreps_here)),
            pltpu.SemaphoreType.DMA((steps, irreps_here)),
            pltpu.SemaphoreType.DMA((n_virt - 1,)),
            pltpu.SemaphoreType.DMA((n_virt - 1,)),
            pltpu.SemaphoreType.DMA((2,)),
        ],
        compiler_params=pltpu.CompilerParams(
            collective_id=0, has_side_effects=True, vmem_limit_bytes=60 * 1024 * 1024
        ),
    )(eri, amplitudes, pairs, eps_virt.reshape(1, nv), virt_counts, pair_counts, eps_occ, eps_virt)
    flat = got.reshape(irreps_here, a_local * BLK, rows)
    update = pl.pallas_call(
        turn_kernel,
        grid=(irreps_here,),
        out_shape=jax.ShapeDtypeStruct((irreps_here, rows, a_local * BLK), jnp.bfloat16),
        in_specs=[pl.BlockSpec((1, a_local * BLK, rows), lambda h: (h, 0, 0))],
        out_specs=pl.BlockSpec((1, rows, a_local * BLK), lambda h: (h, 0, 0)),
        compiler_params=pltpu.CompilerParams(vmem_limit_bytes=60 * 1024 * 1024),
    )(flat)
    return (update, energy)


def solution(mesh):
    placed = (
        P("pair", None, None, None),
        P(None, None, None, ("virt", "pair")),
        P(),
        P(),
        P("pair", None, None),
        P(),
        P(),
    )

    def run(*arrays):
        amplitudes, integrals = arrays[:2]
        loc = integrals.shape[3] // (mesh.shape["virt"] * mesh.shape["pair"])
        whole_slots = loc % amplitudes.shape[3] == 0
        whole_chunks = (integrals.shape[1] // mesh.shape["virt"]) % (2 * A_UNIT) == 0
        body = fused_shards if whole_slots and whole_chunks else shards
        return jax.shard_map(
            body,
            mesh=mesh,
            in_specs=placed,
            out_specs=(P("pair", None, "virt"), P("pair", "virt")),
            check_vma=False,
        )(*arrays)

    return run
```

time: 504 us -> 433 us (0.86)
  local copies, waits for them, and re-layouts: 46.6 us -> 0.57 us
  Pallas kernels: 448 us -> 430 us
    pallas_call x1, Pallas kernels: 448 us -> 419 us  [fused_shards(): pl.pallas_call(functools.partial(ladder_kernel, n_virt, n_pair, irreps_he...]
    reshape x4 -> x0, local copies, waits for them, and re-layouts: 24.2 us -> none  [the longest x1 21.2 us: fused_shards(): flat = got.reshape(irreps_here, a_chunk * cuts * BLK, rows)]
    unnamed x4 -> x3, local copies, waits for them, and re-layouts: 21.6 us -> 0.57 us
    pallas_call x0 -> x1, Pallas kernels: none -> 11.9 us  [fused_shards(): pl.pallas_call(turn_kernel, grid=(irreps_here,), out_shape=jax.ShapeDtype...]
where the time goes in v1:
time: 433 us; the launch traced here: 432 us
  Pallas kernels  430 us (99%)
    pallas_call x1, Pallas kernels, fused_shards(): pl.pallas_call(functools.partial(ladder_kernel, n_virt, n_pair, irreps_he...  419 us
    pallas_call x1, Pallas kernels, fused_shards(): pl.pallas_call(turn_kernel, grid=(irreps_here,), out_shape=jax.ShapeDtype...  11.9 us

profile of v1, /device:TPU:0, one launch (start us, length us, event | category | flops | bytes accessed | tf_op | source)
XLA Modules:
  0.0 431.7 jit_solution(15323805140285993024)
XLA Ops:
  0.6 418.5 %shard_map.86 = (bf16[2,4,16,8,8,1024]{5,4,3,2,1,0:T(8,128)(2,1)}, bf16[32,4,2,2,16,2048]{5,4,3,2,1,0:T(8,128)(2,1)}, f32[2,128]{1,0:T(2,128)}) custom-call(bf16[2,4096,2048]{2,1,0:T(8,128)(2,1)} %bitcast.4, bf16[2,1024,2,1024]{3,2,1,0:T(2,128)(2,1)} %amps_ref.1, s32[2,2,1024]{2,1,0:T(2,128)} %bitcast.6, f32[1,512]{1,0:T(1,128)} %bitcast.7, s32[8]{0:T(128)} %vcount_ref.1, ...), custom_call_target="tpu_custom_call" | custom-call | tf_op jit(solution)/shard_map/pallas_call | solution.py:424
  419.2 0.0 copy-start
  419.2 11.9 %shard_map.87 = bf16[2,1024,4096]{2,1,0:T(8,128)(2,1)} custom-call(bf16[2,4096,1024]{2,1,0:T(8,128)(2,1)} %bitcast.5), custom_call_target="tpu_custom_call" | custom-call | tf_op jit(solution)/shard_map/pallas_call | solution.py:465
  431.1 0.0 copy-done
  431.1 0.6 copy.10
Async XLA Ops:
  419.2 12.0 %copy-start = (f32[2,128]{1,0:T(2,128)S(1)}, f32[2,128]{1,0:T(2,128)}, u32[]{:S(2)}) copy-start(f32[2,128]{1,0:T(2,128)} %get-tuple-element.9) | copy-start | bytes 3076

commit v2 on v1

--- a/solution.py
+++ b/solution.py
@@ -14,6 +14,7 @@
 SLABS = 2
 A_UNIT = 16
 MESH = pl.DeviceIdType.MESH
+TURNS = {(8, 4): (7, 6, 5, 3, 4, 2, 7, 6, 5, 3, 4, 2, 1, 1, 0, 0)}
 
 
 def pick_counts(irrep_ids, table):
@@ -85,17 +86,15 @@
 
 
 def step_plan(count, units):
+    turns = TURNS.get((count, units))
+    if turns is None:
+        turns = [count - 1 - i for _ in range(units // 2) for i in range(count)]
     plan = []
-    for i in range(count):
-        sizes = [2] * (units // 2) + [1] * (units % 2)
-        if i == 0:
-            sizes = [1, 1] + sizes[1:]
-        if i == count - 1 and sizes[-1] == 2:
-            sizes = sizes[:-1] + [1, 1]
-        start = 0
-        for size in sizes:
-            plan.append((count - 1 - i, start, size))
-            start += size
+    used = [0] * count
+    for i, d in enumerate(turns):
+        for size in (1, 1) if i in (0, len(turns) - 1) else (2,):
+            plan.append((d, used[d], size))
+            used[d] += size
     return plan
 
 
@@ -183,7 +182,7 @@
         here = out_buf.at[first_unit[t] : first_unit[t] + size, hh]
         there = got_ref.at[hh, start : start + size, :, me_v]
         if d == 0:
-            return pltpu.make_async_copy(here, there, keep_sem.at[t - (steps - keep_sem.shape[0]), hh])
+            return pltpu.make_async_copy(here, there, keep_sem.at[start, hh])
         return pltpu.make_async_remote_copy(
             src_ref=here,
             dst_ref=there,
@@ -388,15 +387,38 @@
             out_copy(t, hh).wait()
 
 
-def turn_kernel(in_ref, out_ref):
-    size = 256
-    eye = unit_matrix(1, 1, size)
-    for i in range(in_ref.shape[1] // size):
-        for j in range(in_ref.shape[2] // size):
-            block = in_ref[0, i * size : (i + 1) * size, j * size : (j + 1) * size]
-            out_ref[0, j * size : (j + 1) * size, i * size : (i + 1) * size] = lax.dot_general(
-                eye, block, (((1,), (1,)), ((), ())), preferred_element_type=jnp.float32
-            ).astype(jnp.bfloat16)
+def turn_kernel(in_ref, out_ref, turned, sem):
+    irreps_here, units, unit, n_virt, sb_here, rows = in_ref.shape
+    block = turned.shape[1]
+    per_a = n_virt * sb_here
+    group = block // per_a
+    per = rows // block
+    eye = unit_matrix(1, 1, block)
+
+    def out_copy(i):
+        at = pl.multiple_of((i % per) * block, block)
+        return pltpu.make_async_copy(turned.at[i % 2], out_ref.at[i // per, pl.ds(at, block)], sem.at[i % 2])
+
+    def step(i, carry):
+        @pl.when(i >= 2)
+        def _():
+            out_copy(i - 2).wait()
+
+        cols = pl.ds(pl.multiple_of((i % per) * block, block), block)
+        for u in range(units):
+            for a in range(0, unit, group):
+                piece = in_ref[i // per, u, a : a + group, :, :, cols].reshape(block, block)
+                lanes = (u * unit + a) * per_a
+                turned[i % 2, :, lanes : lanes + block] = lax.dot_general(
+                    eye, piece, (((1,), (1,)), ((), ())), preferred_element_type=jnp.float32
+                ).astype(jnp.bfloat16)
+        out_copy(i).start()
+        return carry
+
+    count = irreps_here * per
+    lax.fori_loop(0, count, step, 0)
+    for i in range(max(count - 2, 0), count):
+        out_copy(i).wait()
 
 
 def fused_shards(amplitudes, integrals, virt_counts, pair_counts, pair_list, eps_occ, eps_virt):
@@ -411,7 +433,6 @@
     units = a_local // A_UNIT
     plan = step_plan(n_virt, units)
     steps = len(plan)
-    kept = sum(1 for d, _, _ in plan if d == 0)
     parts_sb = loc // ks
     sb_here = n_pair * parts_sb
     a_rows = 256 // slabs
@@ -424,12 +445,12 @@
     got, _, energy = pl.pallas_call(
         functools.partial(ladder_kernel, n_virt, n_pair, irreps_here, depth, parts_sb, nv * BLK),
         out_shape=(
-            jax.ShapeDtypeStruct((irreps_here, units, A_UNIT, n_virt, sb_here, rows), jnp.bfloat16),
+            pltpu.VMEM((irreps_here, units, A_UNIT, n_virt, sb_here, rows), jnp.bfloat16),
             jax.ShapeDtypeStruct((units * n_virt, n_pair, irreps_here, slabs, A_UNIT, loc), jnp.bfloat16),
             jax.ShapeDtypeStruct((irreps_here, rows // n_virt), jnp.float32),
         ),
         in_specs=[hbm, hbm, vmem, vmem, smem, smem, smem, smem],
-        out_specs=(hbm, hbm, vmem),
+        out_specs=(vmem, hbm, vmem),
         scratch_shapes=[
             pltpu.VMEM((slabs, 2 * A_UNIT * irreps, loc), jnp.bfloat16),
             pltpu.VMEM((depth, 2, n_pair, irreps_here, slabs, A_UNIT, loc), jnp.bfloat16),
@@ -448,7 +469,7 @@
             pltpu.SemaphoreType.DMA,
             pltpu.SemaphoreType.DMA,
             pltpu.SemaphoreType.DMA((depth,)),
-            pltpu.SemaphoreType.DMA((kept, irreps_here)),
+            pltpu.SemaphoreType.DMA((units, irreps_here)),
             pltpu.SemaphoreType.DMA((depth, n_pair - 1)),
             pltpu.SemaphoreType.DMA((steps, n_pair - 1)),
             pltpu.SemaphoreType.DMA((steps, irreps_here)),
@@ -458,18 +479,20 @@
             pltpu.SemaphoreType.DMA((2,)),
         ],
         compiler_params=pltpu.CompilerParams(
-            collective_id=0, has_side_effects=True, vmem_limit_bytes=60 * 1024 * 1024
+            collective_id=0, has_side_effects=True, vmem_limit_bytes=44 * 1024 * 1024
         ),
     )(eri, amplitudes, pairs, eps_virt.reshape(1, nv), virt_counts, pair_counts, eps_occ, eps_virt)
-    flat = got.reshape(irreps_here, a_local * BLK, rows)
     update = pl.pallas_call(
         turn_kernel,
-        grid=(irreps_here,),
         out_shape=jax.ShapeDtypeStruct((irreps_here, rows, a_local * BLK), jnp.bfloat16),
-        in_specs=[pl.BlockSpec((1, a_local * BLK, rows), lambda h: (h, 0, 0))],
-        out_specs=pl.BlockSpec((1, rows, a_local * BLK), lambda h: (h, 0, 0)),
-        compiler_params=pltpu.CompilerParams(vmem_limit_bytes=60 * 1024 * 1024),
-    )(flat)
+        in_specs=[vmem],
+        out_specs=hbm,
+        scratch_shapes=[
+            pltpu.VMEM((2, 256, a_local * BLK), jnp.bfloat16),
+            pltpu.SemaphoreType.DMA((2,)),
+        ],
+        compiler_params=pltpu.CompilerParams(vmem_limit_bytes=12 * 1024 * 1024),
+    )(pltpu.with_memory_space_constraint(got, pltpu.VMEM))
     return (update, energy)
 
 

time: 433 us -> 408 us (0.942)
  Pallas kernels: 430 us -> 406 us
    pallas_call x1, Pallas kernels: 419 us -> 397 us  [fused_shards(): pl.pallas_call(functools.partial(ladder_kernel, n_virt, n_pair, irreps_he...]
where the time goes in v2:
time: 408 us; the launch traced here: 407 us
  Pallas kernels  406 us (100%)
    pallas_call x1, Pallas kernels, fused_shards(): pl.pallas_call(functools.partial(ladder_kernel, n_virt, n_pair, irreps_he...  397 us
    pallas_call x1, Pallas kernels, fused_shards(): pl.pallas_call(turn_kernel, out_shape=jax.ShapeDtypeStruct((irreps_here,...  9.12 us

profile of v2, /device:TPU:0, one launch (start us, length us, event | category | flops | bytes accessed | tf_op | source)
XLA Modules:
  0.0 407.0 jit_solution(18218779559337864551)
XLA Ops:
  0.6 396.7 %shard_map.86 = (bf16[2,4,16,8,8,1024]{5,4,3,2,1,0:T(8,128)(2,1)S(1)}, bf16[32,4,2,2,16,2048]{5,4,3,2,1,0:T(8,128)(2,1)}, f32[2,128]{1,0:T(2,128)}) custom-call(bf16[2,4096,2048]{2,1,0:T(8,128)(2,1)} %bitcast.3, bf16[2,1024,2,1024]{3,2,1,0:T(2,128)(2,1)} %amps_ref.1, s32[2,2,1024]{2,1,0:T(2,128)} %bitcast.4, f32[1,512]{1,0:T(1,128)} %bitcast.5, ...), custom_call_target="tpu_custom_call" | custom-call | tf_op jit(solution)/shard_map/pallas_call | solution.py:445
  397.3 0.0 copy-start
  397.3 9.1 %shard_map.87 = bf16[2,1024,4096]{2,1,0:T(8,128)(2,1)} custom-call(bf16[2,4,16,8,8,1024]{5,4,3,2,1,0:T(8,128)(2,1)S(1)} %get-tuple-element.4.in_ref), custom_call_target="tpu_custom_call" | custom-call | tf_op jit(solution)/shard_map/pallas_call | solution.py:485
  406.4 0.0 copy-done
  406.5 0.6 copy.10
Async XLA Ops:
  397.3 9.1 %copy-start = (f32[2,128]{1,0:T(2,128)S(1)}, f32[2,128]{1,0:T(2,128)}, u32[]{:S(2)}) copy-start(f32[2,128]{1,0:T(2,128)} %get-tuple-element.9) | copy-start | bytes 3076

commit v3 on v2

--- a/solution.py
+++ b/solution.py
@@ -14,7 +14,7 @@
 SLABS = 2
 A_UNIT = 16
 MESH = pl.DeviceIdType.MESH
-TURNS = {(8, 4): (7, 6, 5, 3, 4, 2, 7, 6, 5, 3, 4, 2, 1, 1, 0, 0)}
+TURNS = {8: (7, 2, 6, 3, 5, 4, 1, 0)}
 
 
 def pick_counts(irrep_ids, table):
@@ -85,17 +85,8 @@
     return flipped
 
 
-def step_plan(count, units):
-    turns = TURNS.get((count, units))
-    if turns is None:
-        turns = [count - 1 - i for _ in range(units // 2) for i in range(count)]
-    plan = []
-    used = [0] * count
-    for i, d in enumerate(turns):
-        for size in (1, 1) if i in (0, len(turns) - 1) else (2,):
-            plan.append((d, used[d], size))
-            used[d] += size
-    return plan
+def turn_order(count):
+    return TURNS.get(count, tuple(range(count - 1, -1, -1)))
 
 
 def unit_matrix(count, outer, inner):
@@ -127,28 +118,21 @@
     unit_rows = A_UNIT * irreps
     sb_here = n_pair * parts_sb
     out_rows = A_UNIT * sb_here
-    plan = step_plan(n_virt, a_local // A_UNIT)
-    steps = len(plan)
+    order = turn_order(n_virt)
+    rounds = a_local // A_UNIT
     e_cols = nrows // n_virt
     tile_n = 512
-    tile_r = 256
+    tile_m = 256
+    tile_r = 512
     a_rows = a_buf.shape[1]
     peers = [d for d in range(2, n_pair)] + [1]
-    first_unit = []
-    total = 0
-    for _, _, size in plan:
-        first_unit.append(total)
-        total += size
-
-    def target(t):
-        return flip_bits(me_v, plan[t][0], n_virt)
-
-    def x_copy(t):
-        _, start, size = plan[t]
-        at = pl.multiple_of((target(t) * (a_local // A_UNIT) + start) * unit_rows, unit_rows)
-        return pltpu.make_async_copy(
-            eri_ref.at[:, pl.ds(at, size * unit_rows), :], x_buf.at[:, 0 : size * unit_rows, :], x_sem
-        )
+
+    def target(i):
+        return flip_bits(me_v, order[i], n_virt)
+
+    def x_copy(r, i):
+        at = pl.multiple_of((target(i) * rounds + r) * unit_rows, unit_rows)
+        return pltpu.make_async_copy(eri_ref.at[:, pl.ds(at, unit_rows), :], x_buf, x_sem)
 
     def a_copy(block):
         per = nrows // a_rows
@@ -157,38 +141,33 @@
             amps_ref.at[block // per, pl.ds(at, a_rows)], a_buf.at[block % 2], a_sem.at[block % 2]
         )
 
-    def pair_copy(t, d):
+    def pair_copy(r, i, d):
         peer = flip_bits(me_p, d, n_pair)
-        size = plan[t][2]
         return pltpu.make_async_remote_copy(
-            src_ref=stage.at[t % depth, 0:size, peer],
-            dst_ref=recv_ref.at[first_unit[t] : first_unit[t] + size, me_p],
-            send_sem=send_sem.at[t % depth, d - 1],
-            recv_sem=recv_sem.at[t, d - 1],
+            src_ref=stage.at[i % depth, peer],
+            dst_ref=recv_ref.at[r * n_virt + i, me_p],
+            send_sem=send_sem.at[i % depth, d - 1],
+            recv_sem=recv_sem.at[r * n_virt + i, d - 1],
             device_id=(me_v, peer),
             device_id_type=MESH,
         )
 
-    def own_copy(t):
-        size = plan[t][2]
+    def own_copy(r, i):
         return pltpu.make_async_copy(
-            stage.at[t % depth, 0:size, me_p],
-            recv_ref.at[first_unit[t] : first_unit[t] + size, me_p],
-            own_sem.at[t % depth],
-        )
-
-    def out_copy(t, hh):
-        d, start, size = plan[t]
-        here = out_buf.at[first_unit[t] : first_unit[t] + size, hh]
-        there = got_ref.at[hh, start : start + size, :, me_v]
-        if d == 0:
-            return pltpu.make_async_copy(here, there, keep_sem.at[start, hh])
+            stage.at[i % depth, me_p], recv_ref.at[r * n_virt + i, me_p], own_sem.at[i % depth]
+        )
+
+    def out_copy(r, i, hh):
+        here = out_buf.at[r * n_virt + i, hh]
+        there = got_ref.at[hh, r, :, me_v]
+        if order[i] == 0:
+            return pltpu.make_async_copy(here, there, keep_sem.at[r, hh])
         return pltpu.make_async_remote_copy(
             src_ref=here,
             dst_ref=there,
-            send_sem=out_sem.at[t, hh],
-            recv_sem=got_sem.at[t, hh],
-            device_id=(target(t), me_p),
+            send_sem=out_sem.at[r * n_virt + i, hh],
+            recv_sem=got_sem.at[r * n_virt + i, hh],
+            device_id=(target(i), me_p),
             device_id_type=MESH,
         )
 
@@ -204,36 +183,38 @@
             device_id_type=MESH,
         )
 
-    def prepare(t):
-        size = plan[t][2]
-        n = size * unit_rows
-        x_copy(t).wait()
-
-        def sort_tile(i, carry):
-            cols = pl.ds(pl.multiple_of(i * tile_n, tile_n), tile_n)
+    def prepare(r, i):
+        x_copy(r, i).wait()
+
+        def sort_tile(k, carry):
+            cols = pl.ds(pl.multiple_of(k * tile_n, tile_n), tile_n)
             for s in range(slabs):
                 sorted_rows = jnp.dot(
-                    sort_in[0:n, 0:n], x_buf[s, 0:n, cols], preferred_element_type=jnp.float32
+                    sort_in[...], x_buf[s, :, cols], preferred_element_type=jnp.float32
                 ).astype(jnp.bfloat16)
-                for u in range(size):
-                    for h in range(irreps):
-                        at = u * unit_rows + h * A_UNIT
-                        stage[
-                            t % depth, u, h // irreps_here, h % irreps_here, s, :, cols
-                        ] = sorted_rows[at : at + A_UNIT]
+                for h in range(irreps):
+                    stage[i % depth, h // irreps_here, h % irreps_here, s, :, cols] = sorted_rows[
+                        h * A_UNIT : (h + 1) * A_UNIT
+                    ]
             return carry
 
         lax.fori_loop(0, loc // tile_n, sort_tile, 0)
-        if t + 1 < steps:
-            x_copy(t + 1).start()
+        if i + 1 < n_virt:
+            x_copy(r, i + 1).start()
+        else:
+
+            @pl.when(r + 1 < rounds)
+            def _():
+                x_copy(r + 1, 0).start()
+
         for d in peers:
-            pair_copy(t, d).start()
-        own_copy(t).start()
+            pair_copy(r, i, d).start()
+        own_copy(r, i).start()
 
     def load_amps(hh):
         per = nrows // a_rows
         h = me_p * irreps_here + hh
-        slot = lax.broadcasted_iota(jnp.int32, (1, tile_r), 1) % BLK
+        slot = lax.broadcasted_iota(jnp.int32, (1, tile_m), 1) % BLK
         dmask = jnp.where(slot < vcount_ref[h], 1.0, 0.0).astype(jnp.bfloat16)
 
         def block(i, carry):
@@ -245,9 +226,9 @@
                 a_copy(now + 1).start()
 
             rows = pl.ds(pl.multiple_of(i * a_rows, a_rows), a_rows)
-            for c in range(ks // tile_r):
-                lanes = slice(c * tile_r, (c + 1) * tile_r)
-                mixed = a_buf[now % 2, :, :, lanes].reshape(a_rows * slabs, tile_r)
+            for c in range(ks // tile_m):
+                lanes = slice(c * tile_m, (c + 1) * tile_m)
+                mixed = a_buf[now % 2, :, :, lanes].reshape(a_rows * slabs, tile_m)
                 split = jnp.dot(pick[0], mixed, preferred_element_type=jnp.float32).astype(jnp.bfloat16) * dmask
                 turned = lax.dot_general(
                     pick[1], split, (((1,), (1,)), ((), ())), preferred_element_type=jnp.float32
@@ -258,69 +239,56 @@
 
         lax.fori_loop(0, per, block, 0)
 
-    def fetch(t):
-        size = plan[t][2]
+    def fetch(r, i):
         for d in range(1, n_pair):
-            pair_copy(t, d).wait_recv()
-        own_copy(t).wait()
-        load = pltpu.make_async_copy(
-            recv_ref.at[first_unit[t] : first_unit[t] + size], y_buf.at[0:size], y_sem
-        )
+            pair_copy(r, i, d).wait_recv()
+        own_copy(r, i).wait()
+        load = pltpu.make_async_copy(recv_ref.at[r * n_virt + i], y_buf, y_sem)
         load.start()
         load.wait()
 
-    def compute(t, hh):
-        _, start, size = plan[t]
-        n = size * out_rows
+    def compute(r, i, hh):
         h = me_p * irreps_here + hh
+        a_first = target(i) * a_local + r * A_UNIT
+        a_irrep = a_first // BLK
+        b_irrep = flip_bits(a_irrep, h, irreps)
+        eps_a = levels[pl.ds(pl.multiple_of(a_first, A_UNIT), A_UNIT), 0:1]
+        a_slot = a_first % BLK + lax.broadcasted_iota(jnp.int32, (A_UNIT, 1), 0)
+        live_a = jnp.where(a_slot < vcount_ref[a_irrep], 1.0, 0.0)
         bases = []
         lives = []
-        for u in range(size):
-            a_first = target(t) * a_local + (start + u) * A_UNIT
-            a_irrep = a_first // BLK
-            b_irrep = flip_bits(a_irrep, h, irreps)
-            eps_a = levels[pl.ds(pl.multiple_of(a_first, A_UNIT), A_UNIT), 0:1]
-            a_slot = a_first % BLK + lax.broadcasted_iota(jnp.int32, (A_UNIT, 1), 0)
-            live_a = jnp.where(a_slot < vcount_ref[a_irrep], 1.0, 0.0)
-            for b in range(sb_here):
-                b_slot = me_v * sb_here + b
-                bases.append(eps_a + evirt_ref[b_irrep * BLK + b_slot])
-                lives.append(live_a * jnp.where(b_slot < vcount_ref[b_irrep], 1.0, 0.0))
-        cols_buf[0, 0:n, :] = jnp.concatenate(bases, axis=0)
-        cols_buf[1, 0:n, :] = jnp.concatenate(lives, axis=0)
-
-        def tile(i, carry):
-            cols = pl.ds(pl.multiple_of(i * tile_r, tile_r), tile_r)
+        for b in range(sb_here):
+            b_slot = me_v * sb_here + b
+            bases.append(eps_a + evirt_ref[b_irrep * BLK + b_slot])
+            lives.append(live_a * jnp.where(b_slot < vcount_ref[b_irrep], 1.0, 0.0))
+        cols_buf[0] = jnp.concatenate(bases, axis=0)
+        cols_buf[1] = jnp.concatenate(lives, axis=0)
+
+        def tile(k, carry):
+            cols = pl.ds(pl.multiple_of(k * tile_r, tile_r), tile_r)
             ladder = None
             for s in range(slabs):
                 left = jnp.concatenate(
-                    [
-                        y_buf[u, p, hh, s, :, j * ks : (j + 1) * ks]
-                        for u in range(size)
-                        for p in range(n_pair)
-                        for j in range(parts_sb)
-                    ],
+                    [y_buf[p, hh, s, :, j * ks : (j + 1) * ks] for p in range(n_pair) for j in range(parts_sb)],
                     axis=0,
                 )
                 term = jnp.dot(left, amps[hh, s, :, cols], preferred_element_type=jnp.float32)
                 ladder = term if ladder is None else ladder + term
-            denom = cols_buf[0, 0:n, :] - occ[hh : hh + 1, cols]
-            live = cols_buf[1, 0:n, :] * occ[irreps_here + hh : irreps_here + hh + 1, cols]
+            denom = cols_buf[0] - occ[hh : hh + 1, cols]
+            live = cols_buf[1] * occ[irreps_here + hh : irreps_here + hh + 1, cols]
             ratio = jnp.where(live > 0.5, ladder / denom, 0.0)
             terms[hh : hh + 1, cols] += jnp.sum(ratio * ladder, axis=0, keepdims=True)
             update = jnp.dot(
-                sort_out[0:n, 0:n], ratio.astype(jnp.bfloat16), preferred_element_type=jnp.float32
+                sort_out[...], ratio.astype(jnp.bfloat16), preferred_element_type=jnp.float32
             ).astype(jnp.bfloat16)
-            out_buf[first_unit[t] : first_unit[t] + size, hh, :, :, cols] = update.reshape(
-                size, A_UNIT, sb_here, tile_r
-            )
+            out_buf[r * n_virt + i, hh, :, :, cols] = update.reshape(A_UNIT, sb_here, tile_r)
             return carry
 
         lax.fori_loop(0, nrows // tile_r, tile, 0)
-        out_copy(t, hh).start()
+        out_copy(r, i, hh).start()
 
     def tables():
-        sort_out[...] = unit_matrix(2, A_UNIT, sb_here)
+        sort_out[...] = unit_matrix(1, A_UNIT, sb_here)
         for i in range(nv // 128):
             piece = jnp.broadcast_to(row_ref[0:1, i * 128 : (i + 1) * 128], (128, 128))
             levels[i * 128 : (i + 1) * 128, :] = piece.T
@@ -336,44 +304,55 @@
             live = slot < pcount_ref[me_p * irreps_here + hh]
             occ[irreps_here + hh : irreps_here + hh + 1, :] = jnp.where(live, 1.0, 0.0)
         pick[0] = unit_matrix(1, slabs, a_rows)
-        pick[1] = unit_matrix(1, 1, tile_r)
+        pick[1] = unit_matrix(1, 1, tile_m)
         terms[...] = jnp.zeros_like(terms)
 
-    x_copy(0).start()
+    x_copy(0, 0).start()
     a_copy(0).start()
     barrier = pltpu.get_barrier_semaphore()
     for d in range(1, n_pair):
         pl.semaphore_signal(barrier, inc=1, device_id=(me_v, flip_bits(me_p, d, n_pair)), device_id_type=MESH)
     for d in range(1, n_virt):
         pl.semaphore_signal(barrier, inc=1, device_id=(flip_bits(me_v, d, n_virt), me_p), device_id_type=MESH)
-    sort_in[...] = unit_matrix(2, irreps, A_UNIT)
+    sort_in[...] = unit_matrix(1, irreps, A_UNIT)
     pl.semaphore_wait(barrier, n_pair - 1 + n_virt - 1)
 
-    ahead = 0
-    while ahead < 2:
-        prepare(ahead)
-        ahead += 1
+    early = depth - irreps_here
+    for i in range(early):
+        prepare(0, i)
     tables()
-    for hh in range(irreps_here):
-        load_amps(hh)
-        if hh == 0:
-            fetch(0)
-        compute(0, hh)
-        if ahead < depth:
-            prepare(ahead)
-            ahead += 1
-    while ahead < depth:
-        prepare(ahead)
-        ahead += 1
-    for t in range(steps):
-        if t > 0:
-            fetch(t)
+
+    def one_round(r, carry):
+        for i in range(n_virt):
             for hh in range(irreps_here):
-                compute(t, hh)
-        for d in range(1, n_pair):
-            pair_copy(t, d).wait_send()
-        if t + depth < steps:
-            prepare(t + depth)
+                if i == 0:
+
+                    @pl.when(r == 0)
+                    def _():
+                        load_amps(hh)
+
+                if hh == 0:
+                    fetch(r, i)
+                compute(r, i, hh)
+                if i == 0:
+
+                    @pl.when(r == 0)
+                    def _():
+                        prepare(0, early + hh)
+
+            for d in range(1, n_pair):
+                pair_copy(r, i, d).wait_send()
+            if i + depth < n_virt:
+                prepare(r, i + depth)
+            else:
+
+                @pl.when(r + 1 < rounds)
+                def _():
+                    prepare(r + 1, i + depth - n_virt)
+
+        return carry
+
+    lax.fori_loop(0, rounds, one_round, 0)
     for d in range(1, n_virt):
         part_copy(d).start()
     for d in range(1, n_virt):
@@ -382,9 +361,14 @@
     for d in range(1, n_virt):
         mine = mine + parts[d - 1]
     energy_ref[...] = mine / energy_scale
-    for t in range(steps):
-        for hh in range(irreps_here):
-            out_copy(t, hh).wait()
+
+    def drain(r, carry):
+        for i in range(n_virt):
+            for hh in range(irreps_here):
+                out_copy(r, i, hh).wait()
+        return carry
+
+    lax.fori_loop(0, rounds, drain, 0)
 
 
 def turn_kernel(in_ref, out_ref, turned, sem):
@@ -409,9 +393,12 @@
             for a in range(0, unit, group):
                 piece = in_ref[i // per, u, a : a + group, :, :, cols].reshape(block, block)
                 lanes = (u * unit + a) * per_a
-                turned[i % 2, :, lanes : lanes + block] = lax.dot_general(
-                    eye, piece, (((1,), (1,)), ((), ())), preferred_element_type=jnp.float32
-                ).astype(jnp.bfloat16)
+                if (a // group) % 2:
+                    turned[i % 2, :, lanes : lanes + block] = piece.T
+                else:
+                    turned[i % 2, :, lanes : lanes + block] = lax.dot_general(
+                        eye, piece, (((1,), (1,)), ((), ())), preferred_element_type=jnp.float32
+                    ).astype(jnp.bfloat16)
         out_copy(i).start()
         return carry
 
@@ -431,8 +418,7 @@
     depth = 4
     a_local = nv // n_virt
     units = a_local // A_UNIT
-    plan = step_plan(n_virt, units)
-    steps = len(plan)
+    steps = n_virt * units
     parts_sb = loc // ks
     sb_here = n_pair * parts_sb
     a_rows = 256 // slabs
@@ -452,18 +438,18 @@
         in_specs=[hbm, hbm, vmem, vmem, smem, smem, smem, smem],
         out_specs=(vmem, hbm, vmem),
         scratch_shapes=[
-            pltpu.VMEM((slabs, 2 * A_UNIT * irreps, loc), jnp.bfloat16),
-            pltpu.VMEM((depth, 2, n_pair, irreps_here, slabs, A_UNIT, loc), jnp.bfloat16),
-            pltpu.VMEM((2, n_pair, irreps_here, slabs, A_UNIT, loc), jnp.bfloat16),
+            pltpu.VMEM((slabs, A_UNIT * irreps, loc), jnp.bfloat16),
+            pltpu.VMEM((depth, n_pair, irreps_here, slabs, A_UNIT, loc), jnp.bfloat16),
+            pltpu.VMEM((n_pair, irreps_here, slabs, A_UNIT, loc), jnp.bfloat16),
             pltpu.VMEM((units * n_virt, irreps_here, A_UNIT, sb_here, rows), jnp.bfloat16),
             pltpu.VMEM((2, a_rows, slabs, ks), jnp.bfloat16),
             pltpu.VMEM((irreps_here, slabs, ks, rows), jnp.bfloat16),
-            pltpu.VMEM((2 * A_UNIT * irreps, 2 * A_UNIT * irreps), jnp.bfloat16),
-            pltpu.VMEM((2 * A_UNIT * sb_here, 2 * A_UNIT * sb_here), jnp.bfloat16),
+            pltpu.VMEM((A_UNIT * irreps, A_UNIT * irreps), jnp.bfloat16),
+            pltpu.VMEM((A_UNIT * sb_here, A_UNIT * sb_here), jnp.bfloat16),
             pltpu.VMEM((2, 256, 256), jnp.bfloat16),
             pltpu.VMEM((nv, 128), jnp.float32),
             pltpu.VMEM((2 * irreps_here, rows), jnp.float32),
-            pltpu.VMEM((2, 2 * A_UNIT * sb_here, 1), jnp.float32),
+            pltpu.VMEM((2, A_UNIT * sb_here, 1), jnp.float32),
             pltpu.VMEM((irreps_here, rows), jnp.float32),
             pltpu.VMEM((n_virt - 1, irreps_here, rows // n_virt), jnp.float32),
             pltpu.SemaphoreType.DMA,
@@ -511,7 +497,7 @@
         amplitudes, integrals = arrays[:2]
         loc = integrals.shape[3] // (mesh.shape["virt"] * mesh.shape["pair"])
         whole_slots = loc % amplitudes.shape[3] == 0
-        whole_chunks = (integrals.shape[1] // mesh.shape["virt"]) % (2 * A_UNIT) == 0
+        whole_chunks = (integrals.shape[1] // mesh.shape["virt"]) % A_UNIT == 0
         body = fused_shards if whole_slots and whole_chunks else shards
         return jax.shard_map(
             body,

time: 408 us -> 399 us (0.978)
  Pallas kernels: 406 us -> 395 us
    pallas_call x1, Pallas kernels: 397 us -> 387 us  [fused_shards(): pl.pallas_call(functools.partial(ladder_kernel, n_virt, n_pair, irreps_he...]
where the time goes in v3:
time: 399 us; the launch traced here: 396 us
  Pallas kernels  395 us (99%)
    pallas_call x1, Pallas kernels, fused_shards(): pl.pallas_call(functools.partial(ladder_kernel, n_virt, n_pair, irreps_he...  387 us
    pallas_call x1, Pallas kernels, fused_shards(): pl.pallas_call(turn_kernel, out_shape=jax.ShapeDtypeStruct((irreps_here,...  8.07 us

profile of v3, /device:TPU:0, one launch (start us, length us, event | category | flops | bytes accessed | tf_op | source)
XLA Modules:
  0.0 396.5 jit_solution(5484375141018112330)
XLA Ops:
  0.6 387.1 %shard_map.86 = (bf16[2,4,16,8,8,1024]{5,4,3,2,1,0:T(8,128)(2,1)S(1)}, bf16[32,4,2,2,16,2048]{5,4,3,2,1,0:T(8,128)(2,1)}, f32[2,128]{1,0:T(2,128)}) custom-call(bf16[2,4096,2048]{2,1,0:T(8,128)(2,1)} %bitcast.3, bf16[2,1024,2,1024]{3,2,1,0:T(2,128)(2,1)} %amps_ref.1, s32[2,2,1024]{2,1,0:T(2,128)} %bitcast.4, f32[1,512]{1,0:T(1,128)} %bitcast.5, ...), custom_call_target="tpu_custom_call" | custom-call | tf_op jit(solution)/shard_map/pallas_call | solution.py:431
  387.8 0.0 copy-start
  387.8 8.1 %shard_map.87 = bf16[2,1024,4096]{2,1,0:T(8,128)(2,1)} custom-call(bf16[2,4,16,8,8,1024]{5,4,3,2,1,0:T(8,128)(2,1)S(1)} %get-tuple-element.4.in_ref), custom_call_target="tpu_custom_call" | custom-call | tf_op jit(solution)/shard_map/pallas_call | solution.py:471
  395.9 0.0 copy-done
  395.9 0.6 copy.10
Async XLA Ops:
  387.8 8.1 %copy-start = (f32[2,128]{1,0:T(2,128)S(1)}, f32[2,128]{1,0:T(2,128)}, u32[]{:S(2)}) copy-start(f32[2,128]{1,0:T(2,128)} %get-tuple-element.9) | copy-start | bytes 3076

commit v4 on v3

--- a/solution.py
+++ b/solution.py
@@ -14,7 +14,7 @@
 SLABS = 2
 A_UNIT = 16
 MESH = pl.DeviceIdType.MESH
-TURNS = {8: (7, 2, 6, 3, 5, 4, 1, 0)}
+TURNS = {8: (7, 6, 5, 4, 2, 3, 1, 0)}
 
 
 def pick_counts(irrep_ids, table):
@@ -103,7 +103,7 @@
     eri_ref, amps_ref, pair_ref, row_ref, vcount_ref, pcount_ref, eocc_ref, evirt_ref,
     got_ref, recv_ref, energy_ref,
     x_buf, stage, y_buf, out_buf, a_buf, amps, sort_in, sort_out, pick, levels, occ, cols_buf, terms, parts,
-    x_sem, y_sem, own_sem, keep_sem, send_sem, recv_sem, out_sem, got_sem, term_sem, part_sem, a_sem,
+    x_sem, y_sem, own_sem, keep_sem, send_sem, recv_sem, out_sem, got_sem, term_sem, part_sem, a_sem, first_sem,
 ):
     me_v = lax.axis_index("virt")
     me_p = lax.axis_index("pair")
@@ -152,6 +152,17 @@
             device_id_type=MESH,
         )
 
+    def first_copy(hh, d):
+        peer = flip_bits(me_p, d, n_pair)
+        return pltpu.make_async_remote_copy(
+            src_ref=stage.at[0, peer, hh],
+            dst_ref=recv_ref.at[0, me_p, hh],
+            send_sem=send_sem.at[0, d - 1],
+            recv_sem=first_sem.at[hh, d - 1],
+            device_id=(me_v, peer),
+            device_id_type=MESH,
+        )
+
     def own_copy(r, i):
         return pltpu.make_async_copy(
             stage.at[i % depth, me_p], recv_ref.at[r * n_virt + i, me_p], own_sem.at[i % depth]
@@ -183,7 +194,7 @@
             device_id_type=MESH,
         )
 
-    def prepare(r, i):
+    def prepare(r, i, first=False):
         x_copy(r, i).wait()
 
         def sort_tile(k, carry):
@@ -207,8 +218,13 @@
             def _():
                 x_copy(r + 1, 0).start()
 
-        for d in peers:
-            pair_copy(r, i, d).start()
+        if first:
+            for hh in range(irreps_here):
+                for d in peers:
+                    first_copy(hh, d).start()
+        else:
+            for d in peers:
+                pair_copy(r, i, d).start()
         own_copy(r, i).start()
 
     def load_amps(hh):
@@ -244,6 +260,15 @@
             pair_copy(r, i, d).wait_recv()
         own_copy(r, i).wait()
         load = pltpu.make_async_copy(recv_ref.at[r * n_virt + i], y_buf, y_sem)
+        load.start()
+        load.wait()
+
+    def fetch_first(hh):
+        for d in range(1, n_pair):
+            first_copy(hh, d).wait_recv()
+        if hh == 0:
+            own_copy(0, 0).wait()
+        load = pltpu.make_async_copy(recv_ref.at[0, :, hh], y_buf.at[:, hh], y_sem)
         load.start()
         load.wait()
 
@@ -315,12 +340,10 @@
     for d in range(1, n_virt):
         pl.semaphore_signal(barrier, inc=1, device_id=(flip_bits(me_v, d, n_virt), me_p), device_id_type=MESH)
     sort_in[...] = unit_matrix(1, irreps, A_UNIT)
+    tables()
     pl.semaphore_wait(barrier, n_pair - 1 + n_virt - 1)
 
-    early = depth - irreps_here
-    for i in range(early):
-        prepare(0, i)
-    tables()
+    prepare(0, 0, first=True)
 
     def one_round(r, carry):
         for i in range(n_virt):
@@ -330,15 +353,26 @@
                     @pl.when(r == 0)
                     def _():
                         load_amps(hh)
-
-                if hh == 0:
+                        fetch_first(hh)
+
+                    if hh == 0:
+
+                        @pl.when(r > 0)
+                        def _():
+                            fetch(r, i)
+
+                elif hh == 0:
                     fetch(r, i)
                 compute(r, i, hh)
                 if i == 0:
 
                     @pl.when(r == 0)
                     def _():
-                        prepare(0, early + hh)
+                        if hh + 1 < irreps_here:
+                            prepare(0, hh + 1)
+                        else:
+                            for k in range(hh + 1, depth):
+                                prepare(0, k)
 
             for d in range(1, n_pair):
                 pair_copy(r, i, d).wait_send()
@@ -371,9 +405,9 @@
     lax.fori_loop(0, rounds, drain, 0)
 
 
-def turn_kernel(in_ref, out_ref, turned, sem):
+def turn_kernel(in_ref, energy_ref, out_ref, energy_out, turned, sem):
     irreps_here, units, unit, n_virt, sb_here, rows = in_ref.shape
-    block = turned.shape[1]
+    slots, block = turned.shape[:2]
     per_a = n_virt * sb_here
     group = block // per_a
     per = rows // block
@@ -381,12 +415,12 @@
 
     def out_copy(i):
         at = pl.multiple_of((i % per) * block, block)
-        return pltpu.make_async_copy(turned.at[i % 2], out_ref.at[i // per, pl.ds(at, block)], sem.at[i % 2])
+        return pltpu.make_async_copy(turned.at[i % slots], out_ref.at[i // per, pl.ds(at, block)], sem.at[i % slots])
 
     def step(i, carry):
-        @pl.when(i >= 2)
+        @pl.when(i >= slots)
         def _():
-            out_copy(i - 2).wait()
+            out_copy(i - slots).wait()
 
         cols = pl.ds(pl.multiple_of((i % per) * block, block), block)
         for u in range(units):
@@ -394,17 +428,18 @@
                 piece = in_ref[i // per, u, a : a + group, :, :, cols].reshape(block, block)
                 lanes = (u * unit + a) * per_a
                 if (a // group) % 2:
-                    turned[i % 2, :, lanes : lanes + block] = piece.T
+                    turned[i % slots, :, lanes : lanes + block] = piece.T
                 else:
-                    turned[i % 2, :, lanes : lanes + block] = lax.dot_general(
+                    turned[i % slots, :, lanes : lanes + block] = lax.dot_general(
                         eye, piece, (((1,), (1,)), ((), ())), preferred_element_type=jnp.float32
                     ).astype(jnp.bfloat16)
         out_copy(i).start()
         return carry
 
     count = irreps_here * per
+    energy_out[...] = energy_ref[...]
     lax.fori_loop(0, count, step, 0)
-    for i in range(max(count - 2, 0), count):
+    for i in range(max(count - slots, 0), count):
         out_copy(i).wait()
 
 
@@ -433,7 +468,7 @@
         out_shape=(
             pltpu.VMEM((irreps_here, units, A_UNIT, n_virt, sb_here, rows), jnp.bfloat16),
             jax.ShapeDtypeStruct((units * n_virt, n_pair, irreps_here, slabs, A_UNIT, loc), jnp.bfloat16),
-            jax.ShapeDtypeStruct((irreps_here, rows // n_virt), jnp.float32),
+            pltpu.VMEM((irreps_here, rows // n_virt), jnp.float32),
         ),
         in_specs=[hbm, hbm, vmem, vmem, smem, smem, smem, smem],
         out_specs=(vmem, hbm, vmem),
@@ -463,22 +498,29 @@
             pltpu.SemaphoreType.DMA((n_virt - 1,)),
             pltpu.SemaphoreType.DMA((n_virt - 1,)),
             pltpu.SemaphoreType.DMA((2,)),
+            pltpu.SemaphoreType.DMA((irreps_here, n_pair - 1)),
         ],
         compiler_params=pltpu.CompilerParams(
             collective_id=0, has_side_effects=True, vmem_limit_bytes=44 * 1024 * 1024
         ),
     )(eri, amplitudes, pairs, eps_virt.reshape(1, nv), virt_counts, pair_counts, eps_occ, eps_virt)
-    update = pl.pallas_call(
+    update, energy = pl.pallas_call(
         turn_kernel,
-        out_shape=jax.ShapeDtypeStruct((irreps_here, rows, a_local * BLK), jnp.bfloat16),
-        in_specs=[vmem],
-        out_specs=hbm,
+        out_shape=(
+            jax.ShapeDtypeStruct((irreps_here, rows, a_local * BLK), jnp.bfloat16),
+            jax.ShapeDtypeStruct((irreps_here, rows // n_virt), jnp.float32),
+        ),
+        in_specs=[vmem, vmem],
+        out_specs=(hbm, vmem),
         scratch_shapes=[
-            pltpu.VMEM((2, 256, a_local * BLK), jnp.bfloat16),
-            pltpu.SemaphoreType.DMA((2,)),
+            pltpu.VMEM((3, 256, a_local * BLK), jnp.bfloat16),
+            pltpu.SemaphoreType.DMA((3,)),
         ],
         compiler_params=pltpu.CompilerParams(vmem_limit_bytes=12 * 1024 * 1024),
-    )(pltpu.with_memory_space_constraint(got, pltpu.VMEM))
+    )(
+        pltpu.with_memory_space_constraint(got, pltpu.VMEM),
+        pltpu.with_memory_space_constraint(energy, pltpu.VMEM),
+    )
     return (update, energy)
 
 

time: 399 us -> 397 us (level)
  no operation moved by 1% of the time
where the time goes in v4:
time: 397 us; the launch traced here: 395 us
  Pallas kernels  394 us (99%)
    pallas_call x1, Pallas kernels, fused_shards(): pl.pallas_call(functools.partial(ladder_kernel, n_virt, n_pair, irreps_he...  387 us

profile of v4, /device:TPU:0, one launch (start us, length us, event | category | flops | bytes accessed | tf_op | source)
XLA Modules:
  0.0 395.1 jit_solution(11060090811479679233)
XLA Ops:
  0.6 387.4 %shard_map.86 = (bf16[2,4,16,8,8,1024]{5,4,3,2,1,0:T(8,128)(2,1)S(1)}, bf16[32,4,2,2,16,2048]{5,4,3,2,1,0:T(8,128)(2,1)}, f32[2,128]{1,0:T(2,128)S(1)}) custom-call(bf16[2,4096,2048]{2,1,0:T(8,128)(2,1)} %bitcast.3, bf16[2,1024,2,1024]{3,2,1,0:T(2,128)(2,1)} %amps_ref.1, s32[2,2,1024]{2,1,0:T(2,128)} %bitcast.4, f32[1,512]{1,0:T(1,128)} %bitcast.5, ...), custom_call_target="tpu_custom_call" | custom-call | tf_op jit(solution)/shard_map/pallas_call | solution.py:466
  388.0 7.0 %shard_map.87 = (bf16[2,1024,4096]{2,1,0:T(8,128)(2,1)}, f32[2,128]{1,0:T(2,128)}) custom-call(bf16[2,4,16,8,8,1024]{5,4,3,2,1,0:T(8,128)(2,1)S(1)} %get-tuple-element.4.in_ref, f32[2,128]{1,0:T(2,128)S(1)} %get-tuple-element.5.energy_ref), custom_call_target="tpu_custom_call" | custom-call | tf_op jit(solution)/shard_map/pallas_call | solution.py:507

commit v5 on v4

--- a/solution.py
+++ b/solution.py
@@ -413,14 +413,20 @@
     per = rows // block
     eye = unit_matrix(1, 1, block)
 
-    def out_copy(i):
+    width = unit * per_a
+
+    def out_copy(i, u):
         at = pl.multiple_of((i % per) * block, block)
-        return pltpu.make_async_copy(turned.at[i % slots], out_ref.at[i // per, pl.ds(at, block)], sem.at[i % slots])
+        lanes = slice(u * width, (u + 1) * width)
+        return pltpu.make_async_copy(
+            turned.at[i % slots, :, lanes], out_ref.at[i // per, pl.ds(at, block), lanes], sem.at[i % slots, u]
+        )
 
     def step(i, carry):
         @pl.when(i >= slots)
         def _():
-            out_copy(i - slots).wait()
+            for u in range(units):
+                out_copy(i - slots, u).wait()
 
         cols = pl.ds(pl.multiple_of((i % per) * block, block), block)
         for u in range(units):
@@ -433,14 +439,15 @@
                     turned[i % slots, :, lanes : lanes + block] = lax.dot_general(
                         eye, piece, (((1,), (1,)), ((), ())), preferred_element_type=jnp.float32
                     ).astype(jnp.bfloat16)
-        out_copy(i).start()
+            out_copy(i, u).start()
         return carry
 
     count = irreps_here * per
     energy_out[...] = energy_ref[...]
     lax.fori_loop(0, count, step, 0)
     for i in range(max(count - slots, 0), count):
-        out_copy(i).wait()
+        for u in range(units):
+            out_copy(i, u).wait()
 
 
 def fused_shards(amplitudes, integrals, virt_counts, pair_counts, pair_list, eps_occ, eps_virt):
@@ -514,7 +521,7 @@
         out_specs=(hbm, vmem),
         scratch_shapes=[
             pltpu.VMEM((3, 256, a_local * BLK), jnp.bfloat16),
-            pltpu.SemaphoreType.DMA((3,)),
+            pltpu.SemaphoreType.DMA((3, units)),
         ],
         compiler_params=pltpu.CompilerParams(vmem_limit_bytes=12 * 1024 * 1024),
     )(

time: 397 us -> 397 us (level)
  no operation moved by 1% of the time
where the time goes in v5:
time: 397 us; the launch traced here: 395 us
  Pallas kernels  394 us (99%)
    pallas_call x1, Pallas kernels, fused_shards(): pl.pallas_call(functools.partial(ladder_kernel, n_virt, n_pair, irreps_he...  387 us

profile of v5, /device:TPU:0, one launch (start us, length us, event | category | flops | bytes accessed | tf_op | source)
XLA Modules:
  0.0 394.9 jit_solution(2387752897199444427)
XLA Ops:
  0.6 387.4 %shard_map.86 = (bf16[2,4,16,8,8,1024]{5,4,3,2,1,0:T(8,128)(2,1)S(1)}, bf16[32,4,2,2,16,2048]{5,4,3,2,1,0:T(8,128)(2,1)}, f32[2,128]{1,0:T(2,128)S(1)}) custom-call(bf16[2,4096,2048]{2,1,0:T(8,128)(2,1)} %bitcast.3, bf16[2,1024,2,1024]{3,2,1,0:T(2,128)(2,1)} %amps_ref.1, s32[2,2,1024]{2,1,0:T(2,128)} %bitcast.4, f32[1,512]{1,0:T(1,128)} %bitcast.5, ...), custom_call_target="tpu_custom_call" | custom-call | tf_op jit(solution)/shard_map/pallas_call | solution.py:473
  388.0 6.8 %shard_map.87 = (bf16[2,1024,4096]{2,1,0:T(8,128)(2,1)}, f32[2,128]{1,0:T(2,128)}) custom-call(bf16[2,4,16,8,8,1024]{5,4,3,2,1,0:T(8,128)(2,1)S(1)} %get-tuple-element.4.in_ref, f32[2,128]{1,0:T(2,128)S(1)} %get-tuple-element.5.energy_ref), custom_call_target="tpu_custom_call" | custom-call | tf_op jit(solution)/shard_map/pallas_call | solution.py:514
